TPU v7x, 32 devices: a whole 2x2x4 slice. The times are simulated.
32 devices in a mesh: grp: 2 (over y), row: 4 (over z), col: 4 (over x, core).
Axes of the slice: x: 2, y: 2, z: 4, core: 2. Of those that a mesh axis runs over, the one named last changes fastest.
Arguments:
- activations: bfloat16 [1024, 6144], P(('grp', 'col'), 'row'), parts along dimension 0, may hold values from -6 to 6
- out_grads: bfloat16 [1024, 18432], P(('grp', 'row'), 'col'), parts along dimension 0, may hold values from -0.1796875 to 0.1796875
- matrix: bfloat16 [12288, 18432], P(('grp', 'row'), 'col'), parts along dimension 0, may hold values from -30 to 30
- left: bfloat16 [12288, 256], P(('grp', 'row')), parts along dimension 0, may hold values from -4 to 4
- right: bfloat16 [36864, 256], P(('grp', 'col')), parts along dimension 0, may hold values from -4 to 4
Outputs:
- left_new: bfloat16 [12288, 256], P(('grp', 'row')), parts along dimension 0
- right_new: bfloat16 [36864, 256], P(('grp', 'col')), parts along dimension 0
- residual: bfloat16 [12288, 18432], P(('grp', 'row'), 'col'), parts along dimension 0
There are 2 independent parts, one for each index of `grp`. A program takes and returns all parts, laid end to end along the dimension named above; each array names one. Nothing has to cross between parts.
All inputs are finite; a program needn't handle non-finite values.
Results may differ from a plain program's by a relative error of at most 0.0034.
Values may be sent and summed in bfloat16 or wider, within the bound.
A program may use at most 192 MiB of HBM per device.

v0:
```python
import jax
import jax.numpy as jnp
from jax import lax
from jax.sharding import PartitionSpec as P

epsilon = 1e-06


def contract_rank(first, second):
    return lax.dot_general(
        first, second, (((1,), (1,)), ((), ())), preferred_element_type=jnp.float32
    )


def contract_tokens(first, second):
    return lax.dot_general(
        first, second, (((0,), (0,)), ((), ())), preferred_element_type=jnp.float32
    )


def body(activations, out_grads, matrix, left, right):
    col_count = lax.axis_size("col")
    row_count = lax.axis_size("row")
    gathered = lax.all_gather(activations, "col", axis=0, tiled=True)
    grads_full = lax.all_gather(out_grads, "row", axis=0, tiled=True)
    gradient = contract_tokens(gathered, grads_full)
    wfloat = matrix.astype(jnp.float32)
    fisher = 1.0 + (wfloat * gradient) ** 2
    early_residual = wfloat - contract_rank(left, right)
    weighted_early = (fisher * early_residual).astype(jnp.bfloat16)
    left_partial = jnp.dot(weighted_early, right, preferred_element_type=jnp.float32)
    left_descent = lax.psum(left_partial, "col")
    left_round = left_descent.astype(jnp.bfloat16)
    left_norm_term = jnp.sum(left_descent * left_descent) / col_count
    left_image = contract_rank(left_round, right)
    left_curve, left_norm = lax.psum(
        (jnp.sum(fisher * left_image * left_image), left_norm_term), ("row", "col")
    )
    left_step = left_norm / (left_curve + epsilon)
    left_new = (left.astype(jnp.float32) + left_step * left_descent).astype(jnp.bfloat16)
    later_residual = early_residual - left_step * left_image
    weighted_later = (fisher * later_residual).astype(jnp.bfloat16)
    right_partial = contract_tokens(weighted_later, left_new)
    right_descent = lax.psum(right_partial.astype(jnp.bfloat16), "row").astype(jnp.float32)
    right_round = right_descent.astype(jnp.bfloat16)
    right_norm_term = jnp.sum(right_descent * right_descent) / row_count
    right_image = contract_rank(left_new, right_round)
    right_curve, right_norm = lax.psum(
        (jnp.sum(fisher * right_image * right_image), right_norm_term), ("row", "col")
    )
    right_step = right_norm / (right_curve + epsilon)
    right_new = (right.astype(jnp.float32) + right_step * right_descent).astype(jnp.bfloat16)
    residual = (later_residual - right_step * right_image).astype(jnp.bfloat16)
    return (left_new, right_new, residual)


def solution(mesh):
    placed = (
        P(("grp", "col"), "row"),
        P(("grp", "row"), "col"),
        P(("grp", "row"), "col"),
        P(("grp", "row"), None),
        P(("grp", "col"), None),
    )
    return jax.shard_map(
        body,
        mesh=mesh,
        in_specs=placed,
        out_specs=(P(("grp", "row"), None), P(("grp", "col"), None), P(("grp", "row"), "col")),
        check_vma=False,
    )
```

profile of v0, /device:TPU:0, one launch (start us, length us, event | category | flops | bytes accessed | tf_op | source)
XLA Modules:
  0.0 489.8 jit_solution(9094421947014775079)
XLA Ops:
  7.2 0.0 all-gather.3.cloned.1.call-start
  7.2 0.7 all-gather.3.cloned.1.call-update
  7.9 0.0 all-gather.5.cloned.1.call-start
  7.9 0.7 all-gather.5.cloned.1.call-update
  8.6 0.0 all-reduce.5.cloned.1.call-start
  8.7 19.6 %convert_subtract_fusion = f32[1536,4608]{1,0:T(8,128)} fusion(bf16[1536,4608]{1,0:T(8,128)(2,1)} %param.7, bf16[1536,256]{1,0:T(8,128)(2,1)} %param.8, bf16[4608,256]{1,0:T(8,128)(2,1)} %param.9), kind=kOutput, calls=%fused_computation.2 | convolution fusion | flops 3638034432 | bytes 45613056 | tf_op jit(solution)/shard_map/dot_general | solution.py:10
  28.3 0.0 copy-start
  28.3 3.6 all-gather.3.cloned.1.call-done
  31.9 91.0 %all-gather.5.cloned.1.call-done = bf16[512,4608]{1,0:T(8,128)(2,1)} async-done(((bf16[128,4608]{1,0:T(8,128)(2,1)}), bf16[512,4608]{1,0:T(8,128)(2,1)}) %all-gather.5.cloned.1.call-update) | async-done | bytes 4718608 | tf_op jit(solution)/shard_map/all_gather | solution.py:25
  122.9 17.9 %fusion.1 = f32[1536,4608]{1,0:T(8,128)} fusion(bf16[1536,4608]{1,0:T(8,128)(2,1)} %param.7, bf16[512,1536]{1,0:T(8,128)(2,1)} %all-gather.3.cloned.1.call-done, bf16[512,4608]{1,0:T(8,128)(2,1)} %all-gather.5.cloned.1.call-done), kind=kOutput, calls=%fused_computation.5 | convolution fusion | flops 7276068864 | bytes 48758784 | tf_op jit(solution)/shard_map/dot_general | solution.py:16
  140.8 0.0 copy-done
  140.8 19.9 %fusion.4 = f32[1536,256]{1,0:T(8,128)} fusion(bf16[4608,256]{1,0:T(8,128)(2,1)S(1)} %copy-done, f32[1536,4608]{1,0:T(8,128)} %fusion.1, f32[1536,4608]{1,0:T(8,128)} %convert_subtract_fusion), kind=kOutput, calls=%fused_computation.12 | convolution fusion | flops 3638034432 | bytes 60555264 | tf_op jit(solution)/shard_map/dot_general | solution.py:31
  160.7 0.0 all-reduce.5.cloned.1.call-update
  160.7 0.2 all-reduce.7.cloned.1.call-start
  160.9 41.2 %all-reduce.5.cloned.1.call-done = f32[1536,256]{1,0:T(8,128)} async-done(((f32[1536,256]{1,0:T(8,128)}), f32[1536,256]{1,0:T(8,128)}) %all-reduce.5.cloned.1.call-update) | async-done | bytes 1572880 | tf_op jit(solution)/shard_map/psum | solution.py:32
  202.1 2.4 multiply_reduce_fusion
  205.2 23.8 %fusion.2 = (f32[]{:T(128)}, f32[1536,4608]{1,0:T(8,128)}) fusion(f32[1536,4608]{1,0:T(8,128)} %fusion.1, bf16[4608,256]{1,0:T(8,128)(2,1)S(1)} %copy-done, f32[1536,256]{1,0:T(8,128)} %all-reduce.5.cloned.1.call-done), kind=kOutput, calls=%fused_computation.6 | convolution fusion | flops 3645505536 | bytes 60555268 | tf_op jit(solution)/shard_map/dot_general | solution.py:10
  229.0 32.8 %all-reduce.1 = (f32[]{:T(128)}, f32[]{:T(128)}) all-reduce(f32[]{:T(128)S(6)} %div.12, f32[]{:T(128)} %get-tuple-element.7), channel_id=1, replica_groups=mesh['grp'=2,'row'=4,'col'=4] {'row','col'}, use_global_device_ids=true, to_apply=%region_2.0 | all-reduce | flops 2 | bytes 16 | tf_op jit(solution)/shard_map/psum | solution.py:36
  263.1 1.8 add_convert_fusion
  264.9 0.0 copy-start.2
  264.9 30.2 %fusion.6 = bf16[4608,256]{1,0:T(8,128)(2,1)} fusion(bf16[1536,256]{1,0:T(8,128)(2,1)S(1)} %add_convert_fusion, f32[1536,4608]{1,0:T(8,128)} %fusion.1, f32[1536,4608]{1,0:T(8,128)} %convert_subtract_fusion, f32[1536,4608]{1,0:T(8,128)} %get-tuple-element.8, f32[]{:T(128)S(6)} %div.13), kind=kOutput, calls=%fused_computation.14 | convolution fusion | flops 3653369856 | bytes 88080384 | tf_op jit(solution)/shard_map/dot_general | solution.py:16
  295.1 0.0 all-reduce.7.cloned.1.call-update
  295.2 92.0 %all-reduce.7.cloned.1.call-done = bf16[4608,256]{1,0:T(8,128)(2,1)} async-done(((bf16[4608,256]{1,0:T(8,128)(2,1)}), bf16[4608,256]{1,0:T(8,128)(2,1)}) %all-reduce.7.cloned.1.call-update) | async-done | bytes 2359312 | tf_op jit(solution)/shard_map/psum | solution.py:44
  387.2 3.5 fusion.7
  391.3 0.0 copy-done.2
  391.3 23.9 %fusion.3 = (f32[]{:T(128)}, f32[1536,4608]{1,0:T(8,128)}) fusion(f32[1536,4608]{1,0:T(8,128)} %fusion.1, bf16[1536,256]{1,0:T(8,128)(2,1)S(1)} %add_convert_fusion, bf16[4608,256]{1,0:T(8,128)(2,1)} %all-reduce.7.cloned.1.call-done), kind=kOutput, calls=%fused_computation.7 | convolution fusion | flops 3645112320 | bytes 59768836 | tf_op jit(solution)/shard_map/dot_general | solution.py:10
  415.2 32.0 %all-reduce = (f32[]{:T(128)}, f32[]{:T(128)}) all-reduce(f32[]{:T(128)S(6)} %div.14, f32[]{:T(128)} %get-tuple-element.9), channel_id=1, replica_groups=mesh['grp'=2,'row'=4,'col'=4] {'row','col'}, use_global_device_ids=true, to_apply=%region_7.0 | all-reduce | flops 2 | bytes 16 | tf_op jit(solution)/shard_map/psum | solution.py:48
  448.5 0.0 copy-start.1
  448.5 32.5 %subtract_convert_fusion = bf16[1536,4608]{1,0:T(8,128)(2,1)} fusion(f32[1536,4608]{1,0:T(8,128)} %get-tuple-element.10, f32[]{:T(128)S(6)} %div.15, f32[1536,4608]{1,0:T(8,128)} %convert_subtract_fusion, f32[1536,4608]{1,0:T(8,128)} %get-tuple-element.8, f32[]{:T(128)S(6)} %div.13), kind=kLoop, calls=%fused_computation.8 | loop fusion | flops 35389440 | bytes 99090440 | tf_op jit(solution)/shard_map/convert_element_type | solution.py:53
  481.0 0.0 copy-done.1
  481.0 2.3 fusion.9
Async XLA Ops:
  7.2 24.8 %all-gather.3.cloned.1.call-start = ((), (), s32[]{:S(2)}) async-start(), calls=%async_computation | async-start | bytes 1966080 | tf_op jit(solution)/shard_map/all_gather | solution.py:24
  7.9 115.0 %all-gather.5.cloned.1.call-start = ((), (), s32[]{:S(2)}) async-start(), calls=%async_computation.1 | async-start | bytes 5898240 | tf_op jit(solution)/shard_map/all_gather | solution.py:25
  8.6 193.4 %all-reduce.5.cloned.1.call-start = ((), (), s32[]{:S(2)}) async-start(), calls=%async_computation.2 | async-start | bytes 3145728 | tf_op jit(solution)/shard_map/psum | solution.py:32
  28.3 112.5 %copy-start = (bf16[4608,256]{1,0:T(8,128)(2,1)S(1)}, bf16[4608,256]{1,0:T(8,128)(2,1)}, u32[]{:S(2)}) copy-start(bf16[4608,256]{1,0:T(8,128)(2,1)} %param.9) | copy-start | bytes 7077892
  160.7 226.5 %all-reduce.7.cloned.1.call-start = ((), (), s32[]{:S(2)}) async-start(), calls=%async_computation.3 | async-start | bytes 4718592 | tf_op jit(solution)/shard_map/psum | solution.py:44
  264.9 126.4 %copy-start.2 = (bf16[1536,256]{1,0:T(8,128)(2,1)}, bf16[1536,256]{1,0:T(8,128)(2,1)S(1)}, u32[]{:S(2)}) copy-start(bf16[1536,256]{1,0:T(8,128)(2,1)S(1)} %add_convert_fusion) | copy-start | bytes 2359300
  448.5 32.6 %copy-start.1 = (bf16[4608,256]{1,0:T(8,128)(2,1)S(1)}, bf16[4608,256]{1,0:T(8,128)(2,1)}, u32[]{:S(2)}) copy-start(bf16[4608,256]{1,0:T(8,128)(2,1)} %all-reduce.7.cloned.1.call-done) | copy-start | bytes 7077892
Sparse Core Ops, SparseCore 0:
  9.5 22.3 all-gather.2
  33.5 89.3 all-gather.4
  160.8 41.2 all-reduce.4
  295.3 91.8 all-reduce.6
where the time goes:
time: 490 us
  waiting for transfers between devices  229 us (47%)
  matrix products  135 us (28%)
  blocking collectives  64.8 us (13%)
  other arithmetic  42.5 us (9%)
  between operations  17.7 us (4%)
    psum x1, waiting for transfers between devices, body(): lax.psum(right_partial.astype(jnp.bfloat16), 'row').astype(jnp.float32)  92 us
    all_gather x1, waiting for transfers between devices, body(): grads_full = lax.all_gather(out_grads, 'row', axis=0, tiled=True)  91 us
    dot_general x3, matrix products, contract_rank(): lax.dot_general(first, second, (((1,), (1,)), ((), ())), preferred_elemen...  67.3 us
    dot_general x2, matrix products, contract_tokens(): lax.dot_general(first, second, (((0,), (0,)), ((), ())), preferred_elemen...  48.1 us
    psum x1, waiting for transfers between devices, body(): left_descent = lax.psum(left_partial, 'col')  41.2 us
    psum x1, blocking collectives, body(): lax.psum((jnp.sum(fisher * left_image * left_image), left_norm_term), ('r...  32.8 us
    convert_element_type x1, other arithmetic, body(): residual = (later_residual - right_step * right_image).astype(jnp.bfloat16)  32.5 us
    psum x1, blocking collectives, body(): lax.psum((jnp.sum(fisher * right_image * right_image), right_norm_term),...  32 us
  transfers between devices with their start and end apart: 4, of which 4 were waited for; matrix products, arithmetic and copies ran while one was open for 4% of the time, Pallas kernels for 0%

commit v1 on v0

--- a/solution.py
+++ b/solution.py
@@ -41,7 +41,9 @@
     later_residual = early_residual - left_step * left_image
     weighted_later = (fisher * later_residual).astype(jnp.bfloat16)
     right_partial = contract_tokens(weighted_later, left_new)
-    right_descent = lax.psum(right_partial.astype(jnp.bfloat16), "row").astype(jnp.float32)
+    right_descent = jnp.sum(
+        lax.all_gather(right_partial.astype(jnp.bfloat16), "row"), axis=0
+    ).astype(jnp.float32)
     right_round = right_descent.astype(jnp.bfloat16)
     right_norm_term = jnp.sum(right_descent * right_descent) / row_count
     right_image = contract_rank(left_new, right_round)

time: 490 us -> 570 us (1.16)
  waiting for transfers between devices: 229 us -> 301 us
  other arithmetic: 42.5 us -> 51 us
    all_gather x0 -> x1, waiting for transfers between devices: none -> 164 us  [body(): lax.all_gather(right_partial.astype(jnp.bfloat16), 'row')]
    psum x1 -> x0, waiting for transfers between devices: 92 us -> none  [body(): lax.psum(right_partial.astype(jnp.bfloat16), 'row').astype(jnp.float32)]
    reduce_sum x0 -> x1, other arithmetic: none -> 7.13 us  [body(): jnp.sum(lax.all_gather(right_partial.astype(jnp.bfloat16), 'row'), axis=0)]
  transfers between devices with their start and end apart: 4 -> 4, of which waited for: 4 -> 4; matrix products, arithmetic and copies ran while one was open for 4% -> 3% of each run, Pallas kernels for 0% -> 0%
where the time goes in v1:
time: 570 us
  waiting for transfers between devices  301 us (53%)
  matrix products  135 us (24%)
  blocking collectives  63.8 us (11%)
  other arithmetic  51 us (9%)
  between operations  17.6 us (3%)
    all_gather x1, waiting for transfers between devices, body(): lax.all_gather(right_partial.astype(jnp.bfloat16), 'row')  164 us
    all_gather x1, waiting for transfers between devices, body(): grads_full = lax.all_gather(out_grads, 'row', axis=0, tiled=True)  91 us
    dot_general x3, matrix products, contract_rank(): lax.dot_general(first, second, (((1,), (1,)), ((), ())), preferred_elemen...  67.4 us
    dot_general x2, matrix products, contract_tokens(): lax.dot_general(first, second, (((0,), (0,)), ((), ())), preferred_elemen...  48.2 us
    psum x1, waiting for transfers between devices, body(): left_descent = lax.psum(left_partial, 'col')  41.2 us
    psum x1, blocking collectives, body(): lax.psum((jnp.sum(fisher * left_image * left_image), left_norm_term), ('r...  32.8 us
    convert_element_type x1, other arithmetic, body(): residual = (later_residual - right_step * right_image).astype(jnp.bfloat16)  32.4 us
    psum x1, blocking collectives, body(): lax.psum((jnp.sum(fisher * right_image * right_image), right_norm_term),...  31 us
  transfers between devices with their start and end apart: 4, of which 4 were waited for; matrix products, arithmetic and copies ran while one was open for 3% of the time, Pallas kernels for 0%

profile of v1, /device:TPU:0, one launch (start us, length us, event | category | flops | bytes accessed | tf_op | source)
XLA Modules:
  0.0 569.6 jit_solution(9916728342933266504)
XLA Ops:
  7.2 0.0 all-gather.5.cloned.1.call-start
  7.2 0.7 all-gather.5.cloned.1.call-update
  7.9 0.0 all-gather.7.cloned.1.call-start
  7.9 0.7 all-gather.7.cloned.1.call-update
  8.6 0.0 all-reduce.4.cloned.1.call-start
  8.7 19.6 %convert_subtract_fusion = f32[1536,4608]{1,0:T(8,128)} fusion(bf16[1536,4608]{1,0:T(8,128)(2,1)} %param.7, bf16[1536,256]{1,0:T(8,128)(2,1)} %param.8, bf16[4608,256]{1,0:T(8,128)(2,1)} %param.9), kind=kOutput, calls=%fused_computation.2 | convolution fusion | flops 3638034432 | bytes 45613056 | tf_op jit(solution)/shard_map/dot_general | solution.py:10
  28.3 0.0 copy-start
  28.3 3.6 all-gather.5.cloned.1.call-done
  31.9 91.0 %all-gather.7.cloned.1.call-done = bf16[512,4608]{1,0:T(8,128)(2,1)} async-done(((bf16[128,4608]{1,0:T(8,128)(2,1)}), bf16[512,4608]{1,0:T(8,128)(2,1)}) %all-gather.7.cloned.1.call-update) | async-done | bytes 4718608 | tf_op jit(solution)/shard_map/all_gather | solution.py:25
  122.9 17.9 %fusion.1 = f32[1536,4608]{1,0:T(8,128)} fusion(bf16[1536,4608]{1,0:T(8,128)(2,1)} %param.7, bf16[512,1536]{1,0:T(8,128)(2,1)} %all-gather.5.cloned.1.call-done, bf16[512,4608]{1,0:T(8,128)(2,1)} %all-gather.7.cloned.1.call-done), kind=kOutput, calls=%fused_computation.5 | convolution fusion | flops 7276068864 | bytes 48758784 | tf_op jit(solution)/shard_map/dot_general | solution.py:16
  140.8 0.0 copy-done
  140.8 19.9 %fusion.4 = f32[1536,256]{1,0:T(8,128)} fusion(bf16[4608,256]{1,0:T(8,128)(2,1)S(1)} %copy-done, f32[1536,4608]{1,0:T(8,128)} %fusion.1, f32[1536,4608]{1,0:T(8,128)} %convert_subtract_fusion), kind=kOutput, calls=%fused_computation.12 | convolution fusion | flops 3638034432 | bytes 60555264 | tf_op jit(solution)/shard_map/dot_general | solution.py:31
  160.7 0.0 all-reduce.4.cloned.1.call-update
  160.8 0.2 all-gather.9.cloned.1.call-start
  161.0 41.2 %all-reduce.4.cloned.1.call-done = f32[1536,256]{1,0:T(8,128)} async-done(((f32[1536,256]{1,0:T(8,128)}), f32[1536,256]{1,0:T(8,128)}) %all-reduce.4.cloned.1.call-update) | async-done | bytes 1572880 | tf_op jit(solution)/shard_map/psum | solution.py:32
  202.2 2.4 multiply_reduce_fusion
  205.2 23.7 %fusion.2 = (f32[]{:T(128)}, f32[1536,4608]{1,0:T(8,128)}) fusion(f32[1536,4608]{1,0:T(8,128)} %fusion.1, bf16[4608,256]{1,0:T(8,128)(2,1)S(1)} %copy-done, f32[1536,256]{1,0:T(8,128)} %all-reduce.4.cloned.1.call-done), kind=kOutput, calls=%fused_computation.6 | convolution fusion | flops 3645505536 | bytes 60555268 | tf_op jit(solution)/shard_map/dot_general | solution.py:10
  228.9 32.8 %all-reduce.1 = (f32[]{:T(128)}, f32[]{:T(128)}) all-reduce(f32[]{:T(128)S(6)} %div.12, f32[]{:T(128)} %get-tuple-element.7), channel_id=1, replica_groups=mesh['grp'=2,'row'=4,'col'=4] {'row','col'}, use_global_device_ids=true, to_apply=%region_2.0 | all-reduce | flops 2 | bytes 16 | tf_op jit(solution)/shard_map/psum | solution.py:36
  263.1 1.8 add_convert_fusion
  264.8 0.0 copy-start.1
  264.9 30.2 %fusion.6 = bf16[4608,256]{1,0:T(8,128)(2,1)} fusion(bf16[1536,256]{1,0:T(8,128)(2,1)S(1)} %add_convert_fusion, f32[1536,4608]{1,0:T(8,128)} %fusion.1, f32[1536,4608]{1,0:T(8,128)} %convert_subtract_fusion, f32[1536,4608]{1,0:T(8,128)} %get-tuple-element.8, f32[]{:T(128)S(6)} %div.13), kind=kOutput, calls=%fused_computation.14 | convolution fusion | flops 3653369856 | bytes 88080384 | tf_op jit(solution)/shard_map/dot_general | solution.py:16
  295.1 0.0 all-gather.9.cloned.1.call-update
  295.1 164.1 %all-gather.9.cloned.1.call-done = bf16[18432,256]{1,0:T(8,128)(2,1)} async-done(((bf16[4608,256]{1,0:T(8,128)(2,1)}), bf16[18432,256]{1,0:T(8,128)(2,1)}) %all-gather.9.cloned.1.call-update) | async-done | bytes 9437200 | tf_op jit(solution)/shard_map/all_gather | solution.py:45
  459.3 7.1 %reduce_sum.50 = bf16[4608,256]{1,0:T(8,128)(2,1)} reduce(bf16[4,4608,256]{2,1,0:T(8,128)(2,1)} %bitcast.10, bf16[]{:T(256)} %constant.11.clone.1), dimensions={0}, to_apply=%region_5.0 | reduce | flops 3538944 | bytes 11796482 | tf_op jit(solution)/shard_map/reduce_sum | solution.py:44
  466.4 3.5 fusion.7
  469.9 0.0 copy-done.1
  469.9 24.1 %fusion.3 = (f32[]{:T(128)}, f32[1536,4608]{1,0:T(8,128)}) fusion(f32[1536,4608]{1,0:T(8,128)} %fusion.1, bf16[1536,256]{1,0:T(8,128)(2,1)S(1)} %add_convert_fusion, bf16[4608,256]{1,0:T(8,128)(2,1)} %reduce_sum.50), kind=kOutput, calls=%fused_computation.7 | convolution fusion | flops 3645112320 | bytes 59768836 | tf_op jit(solution)/shard_map/dot_general | solution.py:10
  494.6 31.0 %all-reduce = (f32[]{:T(128)}, f32[]{:T(128)}) all-reduce(f32[]{:T(128)S(6)} %div.14, f32[]{:T(128)} %get-tuple-element.9), channel_id=1, replica_groups=mesh['grp'=2,'row'=4,'col'=4] {'row','col'}, use_global_device_ids=true, to_apply=%region_7.0 | all-reduce | flops 2 | bytes 16 | tf_op jit(solution)/shard_map/psum | solution.py:50
  526.9 3.8 fusion.9
  530.7 32.4 %subtract_convert_fusion = bf16[1536,4608]{1,0:T(8,128)(2,1)} fusion(f32[1536,4608]{1,0:T(8,128)} %get-tuple-element.10, f32[]{:T(128)S(6)} %div.15, f32[1536,4608]{1,0:T(8,128)} %convert_subtract_fusion, f32[1536,4608]{1,0:T(8,128)} %get-tuple-element.8, f32[]{:T(128)S(6)} %div.13), kind=kLoop, calls=%fused_computation.8 | loop fusion | flops 35389440 | bytes 99090440 | tf_op jit(solution)/shard_map/convert_element_type | solution.py:55
Async XLA Ops:
  7.2 24.8 %all-gather.5.cloned.1.call-start = ((), (), s32[]{:S(2)}) async-start(), calls=%async_computation | async-start | bytes 1966080 | tf_op jit(solution)/shard_map/all_gather | solution.py:24
  7.9 115.0 %all-gather.7.cloned.1.call-start = ((), (), s32[]{:S(2)}) async-start(), calls=%async_computation.1 | async-start | bytes 5898240 | tf_op jit(solution)/shard_map/all_gather | solution.py:25
  8.6 193.5 %all-reduce.4.cloned.1.call-start = ((), (), s32[]{:S(2)}) async-start(), calls=%async_computation.2 | async-start | bytes 3145728 | tf_op jit(solution)/shard_map/psum | solution.py:32
  28.3 112.5 %copy-start = (bf16[4608,256]{1,0:T(8,128)(2,1)S(1)}, bf16[4608,256]{1,0:T(8,128)(2,1)}, u32[]{:S(2)}) copy-start(bf16[4608,256]{1,0:T(8,128)(2,1)} %param.9) | copy-start | bytes 7077892
  160.8 298.5 %all-gather.9.cloned.1.call-start = ((), (), s32[]{:S(2)}) async-start(), calls=%async_computation.3 | async-start | bytes 11796480 | tf_op jit(solution)/shard_map/all_gather | solution.py:45
  264.8 205.0 %copy-start.1 = (bf16[1536,256]{1,0:T(8,128)(2,1)}, bf16[1536,256]{1,0:T(8,128)(2,1)S(1)}, u32[]{:S(2)}) copy-start(bf16[1536,256]{1,0:T(8,128)(2,1)S(1)} %add_convert_fusion) | copy-start | bytes 2359300
Sparse Core Ops, SparseCore 0:
  9.5 22.3 all-gather.4
  33.5 89.3 all-gather.6
  160.9 41.2 all-reduce.3
  295.2 163.9 all-gather.8
